TPU v7x, 512 devices: a whole 4x8x8 slice. The times are simulated.
512 devices in a mesh: gx: 32 (over z, x), gy: 16 (over y, core).
Axes of the slice: x: 4, y: 8, z: 8, core: 2. Of those that a mesh axis runs over, the one named last changes fastest.
Arguments:
- probe_seeds: int32 [4], replicated, may hold values from 0 to 1048575
- damping: float32 [2048, 4096], P('gx', 'gy'), may hold values from 0.2 to 1
- coupling_x: float32 [2048, 4096], P('gx', 'gy'), may hold values from 0.05 to 0.5
- coupling_y: float32 [2048, 4096], P('gx', 'gy'), may hold values from 0.05 to 0.5
- sensor_count: int32 [32, 16], P('gx', 'gy'), may hold values from 1 to 256, as said below
- sensor_cells: int32 [32, 16, 256], P('gx', 'gy'), may hold values from 0 to 16383
- obs_weight: float32 [32, 16, 256, 256], P('gx', 'gy'), as said below
Outputs:
- solution: float32 [4, 2048, 4096], P(None, 'gx', 'gy')
- trace_estimate: float32 [], replicated
Inputs may be any that keep to these rules, and one draw needn't show every extreme that they name: `sensor_count`: at most 256, and some block has exactly 256 in every draw; blocks near a few cluster centres are far busier than the rest. `sensor_cells`: cells within the block, numbered row by row. `obs_weight`: each block's matrix is symmetric positive definite.
All inputs are finite; a program needn't handle non-finite values.
Results may differ from a plain program's by a relative error of at most 0.0003.
Values sent between devices are 32-bit elements; how exact they have to be, the bound alone decides.
A program may use at most 64 MiB of HBM per device.

v0:
```python
import jax
import jax.numpy as jnp
from jax import lax
from jax.sharding import Mesh
from jax.sharding import PartitionSpec as P

GX = ("gx_0", "gx_1")
GY = ("gy_0", "gy_1")


tile_rows = 64


def copy_for_each(array, axis):
    devices = lax.axis_size(axis)
    return lax.all_to_all(
        jnp.broadcast_to(array[None], (devices, *array.shape)), axis, 0, 0, tiled=True
    )


def of_everyone(array, axis):
    return copy_for_each(array, axis).sum(axis=0)


def one_axis_at_a_time(array, axes):
    far, near = axes
    return of_everyone(of_everyone(array, near), far)


def with_halo(cells, sides, width):
    for axis, dim in sides:
        count = lax.axis_size(axis)
        head = lax.slice_in_dim(cells, 0, width, axis=dim)
        tail = lax.slice_in_dim(cells, cells.shape[dim] - width, cells.shape[dim], axis=dim)
        cells = jnp.concatenate(
            [
                lax.ppermute(tail, axis, [(i, (i + 1) % count) for i in range(count)]),
                cells,
                lax.ppermute(head, axis, [((i + 1) % count, i) for i in range(count)]),
            ],
            axis=dim,
        )
    return cells


def packed_total(arrays, axis):
    line, at, done = (jnp.concatenate([a.reshape(-1) for a in arrays]), 0, [])
    running = one_axis_at_a_time(line, axis)
    for a in arrays:
        done.append(running[at : at + a.size].reshape(a.shape))
        at += a.size
    return tuple(done)


def rademacher(seeds, row_ids, col_ids):
    mixed = (
        seeds[:, None, None] * 668265261
        + row_ids[None, :, None] * 374761393
        + col_ids[None, None, :] * 1103515245
    )
    mixed = (mixed ^ mixed >> 16 & 65535) * 73244475
    mixed = (mixed ^ mixed >> 16 & 65535) * 73244475
    mixed = mixed ^ mixed >> 16 & 65535
    bit_value = mixed >> 7 & 1
    return (2 * bit_value - 1).astype(jnp.float32)


def apply_region(padded, damping, face_rows, face_cols):
    centre = padded[:, 1:-1, 1:-1]
    return (
        damping * centre
        + face_rows[1:] * (centre - padded[:, 2:, 1:-1])
        + face_rows[:-1] * (centre - padded[:, :-2, 1:-1])
        + face_cols[:, 1:] * (centre - padded[:, 1:-1, 2:])
        + face_cols[:, :-1] * (centre - padded[:, 1:-1, :-2])
    )


def curvature(first, second):
    return one_axis_at_a_time(
        jnp.sum(first * second, axis=(1, 2)), ("gx_0", ("gx_1", "gy_0", "gy_1"))
    )


def per_device(
    probe_seeds, damping, coupling_x, coupling_y, sensor_count, sensor_cells, obs_weight
):
    block_rows, block_cols = damping.shape
    row_ids = lax.axis_index(GX) * block_rows + jnp.arange(block_rows, dtype=jnp.int32)
    col_ids = lax.axis_index(GY) * block_cols + jnp.arange(block_cols, dtype=jnp.int32)
    probes = rademacher(probe_seeds, row_ids, col_ids)
    coefs = with_halo(jnp.stack([damping, coupling_x, coupling_y]), ((GX, 1), (GY, 2)), 2)

    def region(offset):
        reaction = coefs[
            0, 2 - offset : 2 + block_rows + offset, 2 - offset : 2 + block_cols + offset
        ]
        face_rows = coefs[
            1, 1 - offset : 2 + block_rows + offset, 2 - offset : 2 + block_cols + offset
        ]
        face_cols = coefs[
            2, 2 - offset : 2 + block_rows + offset, 1 - offset : 2 + block_cols + offset
        ]
        return (reaction, face_rows, face_cols)

    inner = region(0)
    outer = region(1)
    count = sensor_count[0, 0]
    cell_ids = sensor_cells[0, 0]
    weight = obs_weight[0, 0]
    mask = (jnp.arange(weight.shape[0]) < count).astype(jnp.float32)

    def observe(field):
        flat = field.reshape(field.shape[0], -1)
        sampled = jnp.take(flat, cell_ids, axis=1) * mask
        tiles = (count + tile_rows - 1) // tile_rows

        def add_tile(tile, total):
            start = tile * tile_rows
            left_part = lax.dynamic_slice_in_dim(sampled, start, tile_rows, 1)
            right_part = lax.dynamic_slice_in_dim(weight, start, tile_rows, 0)
            return total + jnp.dot(left_part, right_part, precision=lax.Precision.HIGHEST)

        weighted = lax.fori_loop(0, tiles, add_tile, jnp.zeros_like(sampled))
        weighted = weighted * mask
        return jnp.zeros_like(flat).at[:, cell_ids].add(weighted).reshape(field.shape)

    def operator_twice(field):
        padded = with_halo(field, ((GX, 1), (GY, 2)), 2)
        return apply_region(apply_region(padded, *outer), *inner)

    def hessian(field):
        return operator_twice(field) + observe(field)

    cells_total = block_rows * block_cols * lax.axis_size(GX) * lax.axis_size(GY)
    norm_start = jnp.full((probes.shape[0],), float(cells_total), jnp.float32)
    image = hessian(probes)
    first_step = norm_start / curvature(probes, image)
    solution = first_step[:, None, None] * probes
    residual = probes - first_step[:, None, None] * image
    residual_image = hessian(residual)
    norm_next, product = packed_total(
        (
            jnp.sum(residual * residual, axis=(1, 2)),
            jnp.sum(residual * residual_image, axis=(1, 2)),
        ),
        ("gx_0", ("gx_1", "gy_0", "gy_1")),
    )
    ratio = norm_next / norm_start
    direction = residual + ratio[:, None, None] * probes
    second_step = norm_next / (product - ratio * norm_next / first_step)
    solution = solution + second_step[:, None, None] * direction
    total = one_axis_at_a_time(jnp.sum(probes * solution), ("gx_0", ("gx_1", "gy_0", "gy_1")))
    return (solution, total / probes.shape[0])


def solution(mesh):
    torus = Mesh(mesh.devices.reshape(8, 4, 8, 2), ("gx_0", "gx_1", "gy_0", "gy_1"))
    return jax.shard_map(
        per_device,
        mesh=torus,
        in_specs=(
            P(),
            P(GX, GY),
            P(GX, GY),
            P(GX, GY),
            P(GX, GY),
            P(GX, GY, None),
            P(GX, GY, None, None),
        ),
        out_specs=(P(None, GX, GY), P()),
        check_vma=False,
    )
```

profile of v0, /device:TPU:1, one launch (start us, length us, event | category | flops | bytes accessed | tf_op | source)
XLA Modules:
  0.0 178.7 jit_solution(9362132732724918729)
XLA Ops:
  0.7 0.7 broadcast_multiply_fusion.2
  1.5 0.2 add_convert_fusion.1
  1.7 3.9 %collective-permute-start.4 = (f32[4,2,256]{2,1,0:T(2,128)S(1)}, f32[4,2,256]{2,1,0:T(2,128)S(1)}, u32[]{:S(2)}, u32[]{:S(2)}) collective-permute-start(f32[4,2,256]{2,1,0:T(2,128)S(1)} %get-tuple-element.146), channel_id=1, source_target_pairs={{0,16},{16,32},{32,48},{48,64},{64,80},{80,96},{96,112},{112,128},... | collective-permute-start | bytes 24584 | tf_op jit(solution)/shard_map/ppermute | solution.py:37
  5.6 11.7 %collective-permute-start.5 = (f32[4,2,256]{2,1,0:T(2,128)S(1)}, f32[4,2,256]{2,1,0:T(2,128)S(1)}, u32[]{:S(2)}, u32[]{:S(2)}) collective-permute-start(f32[4,2,256]{2,1,0:T(2,128)S(1)} %get-tuple-element.147), channel_id=1, source_target_pairs={{16,0},{32,16},{48,32},{64,48},{80,64},{96,80},{112,96},{128,112},... | collective-permute-start | bytes 24584 | tf_op jit(solution)/shard_map/ppermute | solution.py:39
  17.3 0.8 pad_maximum_fusion.28
  18.1 1.9 %collective-permute-start = (f32[3,2,256]{2,1,0:T(2,128)S(1)}, f32[3,2,256]{2,1,0:T(2,128)S(1)}, u32[]{:S(2)}, u32[]{:S(2)}) collective-permute-start(f32[3,2,256]{2,1,0:T(2,128)S(1)} %get-tuple-element.150), channel_id=1, source_target_pairs={{0,16},{16,32},{32,48},{48,64},{64,80},{80,96},{96,112},{112,128},... | collective-permute-start | bytes 18440 | tf_op jit(solution)/shard_map/ppermute | solution.py:37
  20.0 6.7 %collective-permute-start.1 = (f32[3,2,256]{2,1,0:T(2,128)S(1)}, f32[3,2,256]{2,1,0:T(2,128)S(1)}, u32[]{:S(2)}, u32[]{:S(2)}) collective-permute-start(f32[3,2,256]{2,1,0:T(2,128)S(1)} %get-tuple-element.151), channel_id=1, source_target_pairs={{16,0},{32,16},{48,32},{64,48},{80,64},{96,80},{112,96},{128,112},... | collective-permute-start | bytes 18440 | tf_op jit(solution)/shard_map/ppermute | solution.py:39
  27.4 0.2 copy.76
  27.6 0.2 add_convert_fusion
  27.8 5.1 %copy.55 = f32[4,16384]{0,1:T(8,128)} copy(f32[4,16384]{1,0:T(4,128)S(1)} %add_convert_fusion) | data formatting | bytes 524288 | tf_op jit(solution)/shard_map/convert_element_type | solution.py:65
  32.9 4.1 %gather_fusion = f32[256,4]{1,0:T(8,128)S(1)} fusion(f32[4,16384]{0,1:T(8,128)} %copy.55, s32[1024]{0:T(1024)S(1)} %pad_clamp_fusion), kind=kCustom, calls=%fused_computation.clone | custom fusion | bytes 9216 | tf_op jit(solution)/shard_map/jit(_take)/gather | solution.py:115
  37.0 0.1 bitcast_multiply_fusion.1
  37.3 0.2 while.20
  37.3 0.2 convolution_add_fusion.4
  37.5 0.1 copy.58
  37.7 5.1 %scatter_custom_fusion = f32[4,16384]{0,1:T(8,128)} fusion(s32[256]{0:T(256)S(1)} %bitcast.67, f32[]{:T(128)} %constant.98.clone.1, f32[4,256]{0,1:T(8,128)S(1)} %copy.58), kind=kCustom, calls=%fused_computation.14 | custom fusion | flops 1024 | bytes 393220 | tf_op jit(solution)/shard_map/scatter-add | solution.py:126
  42.8 5.2 %copy.59 = f32[4,64,256]{2,1,0:T(8,128)S(1)} copy(f32[4,64,256]{0,2,1:T(8,128)} %bitcast.44) | data formatting | bytes 524288 | tf_op jit(solution)/shard_map/reshape | solution.py:126
  48.2 0.1 fusion.65
  48.3 2.7 %collective-permute-start.2 = (f32[3,68,2]{2,1,0:T(8,128)S(1)}, f32[3,68,2]{2,1,0:T(8,128)S(1)}, u32[]{:S(2)}, u32[]{:S(2)}) collective-permute-start(f32[3,68,2]{2,1,0:T(8,128)S(1)} %get-tuple-element.148), channel_id=1, source_target_pairs={{0,1},{1,2},{2,3},{3,4},{4,5},{5,6},{6,7},{7,8},{8,9},{9,10},{10,1... | collective-permute-start | bytes 4904 | tf_op jit(solution)/shard_map/ppermute | solution.py:37
  51.0 1.7 collective-permute-done.2
  52.7 2.4 %collective-permute-done.3 = f32[3,68,2]{2,1,0:T(8,128)S(1)} collective-permute-done((f32[3,68,2]{2,1,0:T(8,128)S(1)}, f32[3,68,2]{2,1,0:T(8,128)S(1)}, u32[]{:S(2)}, u32[]{:S(2)}) %collective-permute-start.3) | collective-permute-done | bytes 1664 | tf_op jit(solution)/shard_map/ppermute | solution.py:39
  55.1 0.2 pad_maximum_fusion.14
  55.3 0.1 slice_bitcast_fusion.3
  55.5 0.1 fusion.66
  55.6 0.1 fusion.58
  55.8 0.1 fusion.62
  55.9 0.5 collective-permute-start.7
  56.4 0.1 fusion.67
  56.5 1.5 collective-permute-done.6
  58.0 2.8 %collective-permute-done.7 = f32[4,68,2]{2,1,0:T(8,128)S(1)} collective-permute-done((f32[4,68,2]{2,1,0:T(8,128)S(1)}, f32[4,68,2]{2,1,0:T(8,128)S(1)}, u32[]{:S(2)}, u32[]{:S(2)}) %collective-permute-start.7) | collective-permute-done | bytes 2208 | tf_op jit(solution)/shard_map/ppermute | solution.py:39
  60.8 0.2 pad_maximum_fusion.12
  61.0 0.6 fusion.22
  61.6 0.5 multiply_reduce_fusion.2
  62.2 18.0 %all_to_all.36 = f32[64,1,4]{2,1,0:T(1,128)S(1)} all-to-all(f32[64,1,4]{2,1,0:T(1,128)S(1)} %broadcast_in_dim.21), channel_id=1, replica_groups=mesh['gx_0'=8,'gx_1'=4,'gy_0'=8,'gy_1'=2] {'gx_1','gy_0','gy_1'}, dimensions={0} | all-to-all | bytes 2048 | tf_op jit(solution)/shard_map/all_to_all | solution.py:16
  80.2 0.1 reduce_sum.91
  80.3 0.6 broadcast_in_dim.22
  80.9 4.1 %all-to-all-start.1 = ((f32[8,1,4]{2,1,0:T(1,128)}), f32[8,1,4]{2,1,0:T(1,128)S(1)}, u32[]{:S(2)}, u32[]{:S(2)}) async-start(f32[8,1,4]{2,1,0:T(1,128)} %broadcast_in_dim.22), calls=%async_computation.1 | async-start | bytes 8192 | tf_op jit(solution)/shard_map/all_to_all | solution.py:16
  85.0 6.5 %all-to-all-done.1 = f32[8,1,4]{2,1,0:T(1,128)S(1)} async-done(((f32[8,1,4]{2,1,0:T(1,128)}), f32[8,1,4]{2,1,0:T(1,128)S(1)}, u32[]{:S(2)}, u32[]{:S(2)}) %all-to-all-start.1) | async-done | bytes 160 | tf_op jit(solution)/shard_map/all_to_all | solution.py:16
  91.5 0.2 multiply_subtract_fusion
  91.7 4.7 %copy.62 = f32[4,64,256]{0,2,1:T(8,128)} copy(f32[4,64,256]{2,1,0:T(8,128)S(1)} %multiply_subtract_fusion) | data formatting | bytes 524288 | tf_op jit(solution)/shard_map/sub | solution.py:140
  96.4 2.3 %collective-permute-start.8 = (f32[4,2,256]{2,1,0:T(2,128)S(1)}, f32[4,2,256]{2,1,0:T(2,128)S(1)}, u32[]{:S(2)}, u32[]{:S(2)}) collective-permute-start(f32[4,2,256]{2,1,0:T(2,128)S(1)} %get-tuple-element.144), channel_id=1, source_target_pairs={{0,16},{16,32},{32,48},{48,64},{64,80},{80,96},{96,112},{112,128},... | collective-permute-start | bytes 24584 | tf_op jit(solution)/shard_map/ppermute | solution.py:37
  98.7 6.3 %collective-permute-start.9 = (f32[4,2,256]{2,1,0:T(2,128)S(1)}, f32[4,2,256]{2,1,0:T(2,128)S(1)}, u32[]{:S(2)}, u32[]{:S(2)}) collective-permute-start(f32[4,2,256]{2,1,0:T(2,128)S(1)} %get-tuple-element.145), channel_id=1, source_target_pairs={{16,0},{32,16},{48,32},{64,48},{80,64},{96,80},{112,96},{128,112},... | collective-permute-start | bytes 24584 | tf_op jit(solution)/shard_map/ppermute | solution.py:39
  105.0 4.1 %gather_fusion.1 = f32[256,4]{1,0:T(8,128)S(1)} fusion(f32[4,16384]{0,1:T(8,128)} %bitcast.45, s32[1024]{0:T(1024)S(1)} %pad_clamp_fusion), kind=kCustom, calls=%fused_computation.1.clone | custom fusion | bytes 9216 | tf_op jit(solution)/shard_map/jit(_take)/gather | solution.py:115
  109.1 0.1 bitcast_multiply_fusion
  109.3 0.2 while.21
  109.3 0.2 convolution_add_fusion.5
  109.6 0.1 fusion.61
  109.7 2.9 %collective-permute-start.10 = (f32[4,68,2]{2,1,0:T(8,128)S(1)}, f32[4,68,2]{2,1,0:T(8,128)S(1)}, u32[]{:S(2)}, u32[]{:S(2)}) collective-permute-start(f32[4,68,2]{2,1,0:T(8,128)S(1)} %get-tuple-element.141), channel_id=1, source_target_pairs={{0,1},{1,2},{2,3},{3,4},{4,5},{5,6},{6,7},{7,8},{8,9},{9,10},{10,1... | collective-permute-start | bytes 6536 | tf_op jit(solution)/shard_map/ppermute | solution.py:37
  112.6 0.1 copy.65
  112.8 5.1 %scatter_custom_fusion.1 = f32[4,16384]{0,1:T(8,128)} fusion(s32[256]{0:T(256)S(1)} %bitcast.68, f32[]{:T(128)} %constant.98.clone.1, f32[4,256]{0,1:T(8,128)S(1)} %copy.65), kind=kCustom, calls=%fused_computation.12 | custom fusion | flops 1024 | bytes 393220 | tf_op jit(solution)/shard_map/scatter-add | solution.py:126
  117.9 5.2 %copy.66 = f32[4,64,256]{2,1,0:T(8,128)S(1)} copy(f32[4,64,256]{0,2,1:T(8,128)} %bitcast.43) | data formatting | bytes 524288 | tf_op jit(solution)/shard_map/reshape | solution.py:126
  123.2 0.2 pad_maximum_fusion.13
  123.4 0.6 fusion.12
  124.0 0.6 multiply_reduce_fusion.1
  124.7 15.4 %all_to_all.37 = f32[64,1,8]{2,1,0:T(1,128)S(1)} all-to-all(f32[64,1,8]{2,1,0:T(1,128)S(1)} %broadcast_in_dim.23), channel_id=1, replica_groups=mesh['gx_0'=8,'gx_1'=4,'gy_0'=8,'gy_1'=2] {'gx_1','gy_0','gy_1'}, dimensions={0} | all-to-all | bytes 4096 | tf_op jit(solution)/shard_map/all_to_all | solution.py:16
  140.1 0.1 reduce_sum.95
  140.2 8.9 %all_to_all.38 = f32[8,1,8]{2,1,0:T(1,128)S(1)} all-to-all(f32[8,1,8]{2,1,0:T(1,128)S(1)} %broadcast_in_dim.24), channel_id=1, replica_groups=mesh['gx_0'=8,'gx_1'=4,'gy_0'=8,'gy_1'=2] {'gx_0'}, dimensions={0} | all-to-all | bytes 512 | tf_op jit(solution)/shard_map/all_to_all | solution.py:16
  149.2 1.6 multiply_reduce_fusion
  150.8 0.7 broadcast_in_dim.25
  151.4 14.7 %all_to_all.39 = f32[64,1,1]{2,1,0:T(1,128)S(1)} all-to-all(f32[64,1,1]{2,1,0:T(1,128)S(1)} %broadcast_in_dim.25), channel_id=1, replica_groups=mesh['gx_0'=8,'gx_1'=4,'gy_0'=8,'gy_1'=2] {'gx_1','gy_0','gy_1'}, dimensions={0} | all-to-all | bytes 512 | tf_op jit(solution)/shard_map/all_to_all | solution.py:16
  166.1 0.7 reduce_sum.98
  166.8 0.6 broadcast_in_dim.26
  167.4 8.9 %all_to_all.40 = f32[8,1,1]{2,1,0:T(1,128)S(1)} all-to-all(f32[8,1,1]{2,1,0:T(1,128)S(1)} %broadcast_in_dim.26), channel_id=1, replica_groups=mesh['gx_0'=8,'gx_1'=4,'gy_0'=8,'gy_1'=2] {'gx_0'}, dimensions={0} | all-to-all | bytes 64 | tf_op jit(solution)/shard_map/all_to_all | solution.py:16
  176.4 0.6 reduce_sum.99
  (51 shorter events, 0.8 us)
Async XLA Ops:
  0.6 32.3 %copy-start.4 = (s32[1,1,256]{2,1,0:T(1,128)S(1)}, s32[1,1,256]{2,1,0:T(1,128)}, u32[]{:S(2)}) copy-start(s32[1,1,256]{2,1,0:T(1,128)} %param.18) | copy-start | bytes 3076
  0.6 36.6 %copy-start.2 = (f32[1,1,256,256]{3,2,1,0:T(8,128)S(1)}, f32[1,1,256,256]{3,2,1,0:T(8,128)}, u32[]{:S(2)}) copy-start(f32[1,1,256,256]{3,2,1,0:T(8,128)} %param.19) | copy-start | bytes 786436
  1.7 54.1 %collective-permute-start.4 = (f32[4,2,256]{2,1,0:T(2,128)S(1)}, f32[4,2,256]{2,1,0:T(2,128)S(1)}, u32[]{:S(2)}, u32[]{:S(2)}) collective-permute-start(f32[4,2,256]{2,1,0:T(2,128)S(1)} %get-tuple-element.146), channel_id=1, source_target_pairs={{0,16},{16,32},{32,48},{48,64},{64,80},{80,96},{96,112},{112,128},... | collective-permute-start | bytes 24584 | tf_op jit(solution)/shard_map/ppermute | solution.py:37
  5.6 50.1 %collective-permute-start.5 = (f32[4,2,256]{2,1,0:T(2,128)S(1)}, f32[4,2,256]{2,1,0:T(2,128)S(1)}, u32[]{:S(2)}, u32[]{:S(2)}) collective-permute-start(f32[4,2,256]{2,1,0:T(2,128)S(1)} %get-tuple-element.147), channel_id=1, source_target_pairs={{16,0},{32,16},{48,32},{64,48},{80,64},{96,80},{112,96},{128,112},... | collective-permute-start | bytes 24584 | tf_op jit(solution)/shard_map/ppermute | solution.py:39
  18.1 30.0 %collective-permute-start = (f32[3,2,256]{2,1,0:T(2,128)S(1)}, f32[3,2,256]{2,1,0:T(2,128)S(1)}, u32[]{:S(2)}, u32[]{:S(2)}) collective-permute-start(f32[3,2,256]{2,1,0:T(2,128)S(1)} %get-tuple-element.150), channel_id=1, source_target_pairs={{0,16},{16,32},{32,48},{48,64},{64,80},{80,96},{96,112},{112,128},... | collective-permute-start | bytes 18440 | tf_op jit(solution)/shard_map/ppermute | solution.py:37
  20.0 28.1 %collective-permute-start.1 = (f32[3,2,256]{2,1,0:T(2,128)S(1)}, f32[3,2,256]{2,1,0:T(2,128)S(1)}, u32[]{:S(2)}, u32[]{:S(2)}) collective-permute-start(f32[3,2,256]{2,1,0:T(2,128)S(1)} %get-tuple-element.151), channel_id=1, source_target_pairs={{16,0},{32,16},{48,32},{64,48},{80,64},{96,80},{112,96},{128,112},... | collective-permute-start | bytes 18440 | tf_op jit(solution)/shard_map/ppermute | solution.py:39
  37.7 10.4 %copy-start = (f32[64,256]{1,0:T(8,128)S(1)}, f32[64,256]{1,0:T(8,128)}, u32[]{:S(2)}) copy-start(f32[64,256]{1,0:T(8,128)} %param.15) | copy-start | bytes 196612
  37.7 10.4 %copy-start.1 = (f32[64,256]{1,0:T(8,128)S(1)}, f32[64,256]{1,0:T(8,128)}, u32[]{:S(2)}) copy-start(f32[64,256]{1,0:T(8,128)} %param.14) | copy-start | bytes 196612
  37.7 10.4 %copy-start.3 = (f32[64,256]{1,0:T(8,128)S(1)}, f32[64,256]{1,0:T(8,128)}, u32[]{:S(2)}) copy-start(f32[64,256]{1,0:T(8,128)} %param.16) | copy-start | bytes 196612
  48.3 4.5 %collective-permute-start.2 = (f32[3,68,2]{2,1,0:T(8,128)S(1)}, f32[3,68,2]{2,1,0:T(8,128)S(1)}, u32[]{:S(2)}, u32[]{:S(2)}) collective-permute-start(f32[3,68,2]{2,1,0:T(8,128)S(1)} %get-tuple-element.148), channel_id=1, source_target_pairs={{0,1},{1,2},{2,3},{3,4},{4,5},{5,6},{6,7},{7,8},{8,9},{9,10},{10,1... | collective-permute-start | bytes 4904 | tf_op jit(solution)/shard_map/ppermute | solution.py:37
  51.0 4.2 %collective-permute-start.3 = (f32[3,68,2]{2,1,0:T(8,128)S(1)}, f32[3,68,2]{2,1,0:T(8,128)S(1)}, u32[]{:S(2)}, u32[]{:S(2)}) collective-permute-start(f32[3,68,2]{2,1,0:T(8,128)S(1)} %get-tuple-element.149), channel_id=1, source_target_pairs={{1,0},{2,1},{3,2},{4,3},{5,4},{6,5},{7,6},{8,7},{9,8},{10,9},{11,1... | collective-permute-start | bytes 4904 | tf_op jit(solution)/shard_map/ppermute | solution.py:39
  55.9 2.1 %collective-permute-start.6 = (f32[4,68,2]{2,1,0:T(8,128)S(1)}, f32[4,68,2]{2,1,0:T(8,128)S(1)}, u32[]{:S(2)}, u32[]{:S(2)}) collective-permute-start(f32[4,68,2]{2,1,0:T(8,128)S(1)} %get-tuple-element.143), channel_id=1, source_target_pairs={{0,1},{1,2},{2,3},{3,4},{4,5},{5,6},{6,7},{7,8},{8,9},{9,10},{10,1... | collective-permute-start | bytes 6536 | tf_op jit(solution)/shard_map/ppermute | solution.py:37
  55.9 4.9 %collective-permute-start.7 = (f32[4,68,2]{2,1,0:T(8,128)S(1)}, f32[4,68,2]{2,1,0:T(8,128)S(1)}, u32[]{:S(2)}, u32[]{:S(2)}) collective-permute-start(f32[4,68,2]{2,1,0:T(8,128)S(1)} %get-tuple-element.142), channel_id=1, source_target_pairs={{1,0},{2,1},{3,2},{4,3},{5,4},{6,5},{7,6},{8,7},{9,8},{10,9},{11,1... | collective-permute-start | bytes 6536 | tf_op jit(solution)/shard_map/ppermute | solution.py:39
  80.9 10.6 %all-to-all-start.1 = ((f32[8,1,4]{2,1,0:T(1,128)}), f32[8,1,4]{2,1,0:T(1,128)S(1)}, u32[]{:S(2)}, u32[]{:S(2)}) async-start(f32[8,1,4]{2,1,0:T(1,128)} %broadcast_in_dim.22), calls=%async_computation.1 | async-start | bytes 8192 | tf_op jit(solution)/shard_map/all_to_all | solution.py:16
  96.4 13.1 %collective-permute-start.8 = (f32[4,2,256]{2,1,0:T(2,128)S(1)}, f32[4,2,256]{2,1,0:T(2,128)S(1)}, u32[]{:S(2)}, u32[]{:S(2)}) collective-permute-start(f32[4,2,256]{2,1,0:T(2,128)S(1)} %get-tuple-element.144), channel_id=1, source_target_pairs={{0,16},{16,32},{32,48},{48,64},{64,80},{80,96},{96,112},{112,128},... | collective-permute-start | bytes 24584 | tf_op jit(solution)/shard_map/ppermute | solution.py:37
  98.7 10.9 %collective-permute-start.9 = (f32[4,2,256]{2,1,0:T(2,128)S(1)}, f32[4,2,256]{2,1,0:T(2,128)S(1)}, u32[]{:S(2)}, u32[]{:S(2)}) collective-permute-start(f32[4,2,256]{2,1,0:T(2,128)S(1)} %get-tuple-element.145), channel_id=1, source_target_pairs={{16,0},{32,16},{48,32},{64,48},{80,64},{96,80},{112,96},{128,112},... | collective-permute-start | bytes 24584 | tf_op jit(solution)/shard_map/ppermute | solution.py:39
  109.7 13.4 %collective-permute-start.10 = (f32[4,68,2]{2,1,0:T(8,128)S(1)}, f32[4,68,2]{2,1,0:T(8,128)S(1)}, u32[]{:S(2)}, u32[]{:S(2)}) collective-permute-start(f32[4,68,2]{2,1,0:T(8,128)S(1)} %get-tuple-element.141), channel_id=1, source_target_pairs={{0,1},{1,2},{2,3},{3,4},{4,5},{5,6},{6,7},{7,8},{8,9},{9,10},{10,1... | collective-permute-start | bytes 6536 | tf_op jit(solution)/shard_map/ppermute | solution.py:37
  112.6 10.5 %collective-permute-start.11 = (f32[4,68,2]{2,1,0:T(8,128)S(1)}, f32[4,68,2]{2,1,0:T(8,128)S(1)}, u32[]{:S(2)}, u32[]{:S(2)}) collective-permute-start(f32[4,68,2]{2,1,0:T(8,128)S(1)} %get-tuple-element.140), channel_id=1, source_target_pairs={{1,0},{2,1},{3,2},{4,3},{5,4},{6,5},{7,6},{8,7},{9,8},{10,9},{11,1... | collective-permute-start | bytes 6536 | tf_op jit(solution)/shard_map/ppermute | solution.py:39
where the time goes:
time: 179 us
  blocking collectives  65.9 us (37%)
  starting transfers between devices  43 us (24%)
  local copies, waits for them, and re-layouts  31.6 us (18%)
  other arithmetic  19.2 us (11%)
  waiting for transfers between devices  15 us (8%)
  between operations  3.57 us (2%)
    all_to_all x5, blocking collectives, copy_for_each(): lax.all_to_all(jnp.broadcast_to(array[None], (devices, *array.shape)), ax...  65.9 us
    ppermute x6, starting transfers between devices, with_halo(): lax.ppermute(head, axis, [((i + 1) % count, i) for i in range(count)])  25.1 us
    ppermute x6, starting transfers between devices, with_halo(): lax.ppermute(tail, axis, [(i, (i + 1) % count) for i in range(count)])  13.8 us
    reshape x2, local copies, waits for them, and re-layouts, observe(): jnp.zeros_like(flat).at[:, cell_ids].add(weighted).reshape(field.shape)  10.5 us
    scatter-add x2, other arithmetic, observe(): jnp.zeros_like(flat).at[:, cell_ids].add(weighted).reshape(field.shape)  10.3 us
    gather x2, local copies, waits for them, and re-layouts, observe(): sampled = jnp.take(flat, cell_ids, axis=1) * mask  8.21 us
    all_to_all x1, waiting for transfers between devices, copy_for_each(): lax.all_to_all(jnp.broadcast_to(array[None], (devices, *array.shape)), ax...  6.48 us
    ppermute x6, waiting for transfers between devices, with_halo(): lax.ppermute(head, axis, [((i + 1) % count, i) for i in range(count)])  5.21 us
  transfers between devices with their start and end apart: 13, of which 5 were waited for; matrix products, arithmetic and copies ran while one was open for 21% of the time, Pallas kernels for 0%

commit v1 on v0

v1 whole, which is shorter than its diff:
```python
import jax
import jax.numpy as jnp
from jax import lax
from jax.experimental import pallas as pl
from jax.experimental.pallas import tpu as pltpu
from jax.sharding import PartitionSpec as P

MESH = pl.DeviceIdType.MESH
NT = (((1,), (1,)), ((), ()))
F32 = jnp.float32
BF16 = jnp.bfloat16

PAD_R, PAD_C = 8, 128


def mix(base):
    mixed = (base ^ ((base >> 16) & 65535)) * 73244475
    mixed = (mixed ^ ((mixed >> 16) & 65535)) * 73244475
    mixed = mixed ^ ((mixed >> 16) & 65535)
    return (2 * ((mixed >> 7) & 1) - 1).astype(F32)


def position(rows, cols):
    return rows * 374761393 + cols * 1103515245


def iota(shape, dim):
    return lax.broadcasted_iota(jnp.int32, shape, dim)


def split3(x):
    high = x.astype(BF16)
    rest = x - high.astype(F32)
    mid = rest.astype(BF16)
    low = (rest - mid.astype(F32)).astype(BF16)
    return high, mid, low


def times(x, y, dims=(((1,), (0,)), ((), ()))):
    total = None
    for part in reversed(split3(x)):
        one = lax.dot_general(part, y, dims, preferred_element_type=F32)
        total = one if total is None else total + one
    return total


def kernel_of(probes, bx, by, rows, cols):
    ext_r, ext_c = rows + 2 * PAD_R, cols + 2 * PAD_C
    nx, ny = bx * rows, by * cols
    r_in = slice(PAD_R, PAD_R + rows)
    c_in = slice(PAD_C, PAD_C + cols)
    first_r, last_r = slice(PAD_R, 2 * PAD_R), slice(rows, PAD_R + rows)
    first_c, last_c = slice(PAD_C, 2 * PAD_C), slice(cols, PAD_C + cols)
    halo_r = {-1: slice(0, PAD_R), 0: r_in, 1: slice(PAD_R + rows, ext_r)}
    halo_c = {-1: slice(0, PAD_C), 0: c_in, 1: slice(PAD_C + cols, ext_c)}
    edge_r = {-1: first_r, 0: r_in, 1: last_r}
    edge_c = {-1: first_c, 0: c_in, 1: last_c}
    near = [(a, b) for a in (-1, 0, 1) for b in (-1, 0, 1) if (a, b) != (0, 0)]
    cross = [(0, 1), (0, -1), (1, 0), (-1, 0)]
    corners = [(a, b) for a in (-1, 1) for b in (-1, 1)]

    def body(seeds_h, damp_h, cx_h, cy_h, count_h, cells_h, weight_h, sol_ref, trace_ref,
             seeds_s, count_s, cells_v, weight_v, coef, up_v, left_v, diag_v, prob, once, image,
             w_send, w_recv, part, got_y, got_x,
             local_sem, coef_send, coef_recv, obs_send, obs_recv, y_send, y_recv, x_send, x_recv):
        gx, gy = lax.axis_index("gx"), lax.axis_index("gy")

        def at(dx, dy):
            return (lax.rem(gx + (dx + bx), bx), lax.rem(gy + (dy + by), by))

        barrier = pltpu.get_barrier_semaphore()
        peers = [(0, d) for d in range(1, by)] + [(d, 0) for d in range(1, bx)] + corners
        for dx, dy in cross + corners:
            pl.semaphore_signal(barrier, inc=1, device_id=at(dx, dy), device_id_type=MESH)
        for dx, dy in peers:
            if (dx, dy) not in corners and (dx, dy) not in ((0, 1), (0, by - 1), (1, 0), (bx - 1, 0)):
                pl.semaphore_signal(barrier, inc=1, device_id=at(dx, dy), device_id_type=MESH)

        loads = [
            pltpu.make_async_copy(damp_h, coef.at[0, r_in, c_in], local_sem.at[0]),
            pltpu.make_async_copy(cx_h, coef.at[1, r_in, c_in], local_sem.at[1]),
            pltpu.make_async_copy(cy_h, coef.at[2, r_in, c_in], local_sem.at[2]),
            pltpu.make_async_copy(cells_h, cells_v, local_sem.at[3]),
            pltpu.make_async_copy(seeds_h, seeds_s, local_sem.at[4]),
            pltpu.make_async_copy(count_h, count_s, local_sem.at[5]),
            pltpu.make_async_copy(weight_h, weight_v, local_sem.at[6]),
        ]
        for load in loads:
            load.start()
        for load in loads[:3]:
            load.wait()
        pl.semaphore_wait(barrier, len(peers))

        sends = []
        for n, (dx, dy) in enumerate(near):
            copy = pltpu.make_async_remote_copy(
                src_ref=coef.at[:, edge_r[dx], edge_c[dy]],
                dst_ref=coef.at[:, halo_r[-dx], halo_c[-dy]],
                send_sem=coef_send.at[n], recv_sem=coef_recv.at[n],
                device_id=at(dx, dy), device_id_type=MESH)
            copy.start()
            sends.append(copy)
        coef_copies = list(sends)

        for load in loads[3:6]:
            load.wait()
        slots = cells_v.shape[1]
        cell = cells_v[...]
        sensor_r = lax.div(cell, cols)
        sensor_c = lax.rem(cell, cols)
        sub = iota((8, slots), 0)
        seed = jnp.where(sub == 0, seeds_s[0, 0], 0)
        for k in range(1, probes):
            seed = jnp.where(sub == k, seeds_s[0, k], seed)
        live = iota((8, slots), 1) < count_s[0, 0]
        keep = jnp.logical_and(live, sub < probes)
        sampled = mix(seed * 668265261 + position(gx * rows + sensor_r, gy * cols + sensor_c))
        sampled = jnp.where(keep, sampled, 0.0)
        loads[6].wait()
        weight = weight_v[...]
        weighted = jnp.dot(sampled, weight, precision=lax.Precision.HIGHEST, preferred_element_type=F32)
        weighted = jnp.where(keep, weighted, 0.0)
        row_f, col_f = sensor_r.astype(F32), sensor_c.astype(F32)
        message = jnp.where(sub == probes, jnp.broadcast_to(row_f, (8, slots)), weighted)
        message = jnp.where(sub == probes + 1, jnp.broadcast_to(col_f, (8, slots)), message)
        w_send[...] = message
        obs_copies = []
        for n, (dx, dy) in enumerate(cross):
            copy = pltpu.make_async_remote_copy(
                src_ref=w_send, dst_ref=w_recv.at[n],
                send_sem=obs_send.at[n], recv_sem=obs_recv.at[n],
                device_id=at(dx, dy), device_id_type=MESH)
            copy.start()
            obs_copies.append(copy)
            sends.append(copy)

        row_ids = (gx * rows - PAD_R + iota((ext_r, ext_c), 0)) & (nx - 1)
        col_ids = (gy * cols - PAD_C + iota((ext_r, ext_c), 1)) & (ny - 1)
        place = position(row_ids, col_ids)
        for k in range(probes):
            prob[k] = mix(seeds_s[0, k] * 668265261 + place)

        in_row = (iota((rows, slots), 0) == sensor_r).astype(F32)
        in_col = (iota((cols, slots), 0) == sensor_c).astype(F32).astype(BF16)
        spread = jnp.concatenate([in_row * weighted[k:k + 1] for k in range(probes)], axis=0)
        own = times(spread, in_col, NT)

        for copy in coef_copies:
            copy.wait_recv()
        damp, cx, cy = coef[0], coef[1], coef[2]
        cxu, cyl = pltpu.roll(cx, 1, 0), pltpu.roll(cy, 1, 1)
        up_v[...] = cxu
        left_v[...] = cyl
        diag_v[...] = damp + cx + cxu + cy + cyl

        def operator(field):
            return (diag_v[...] * field - coef[1] * pltpu.roll(field, ext_r - 1, 0) - up_v[...] * pltpu.roll(field, 1, 0)
                    - coef[2] * pltpu.roll(field, ext_c - 1, 1) - left_v[...] * pltpu.roll(field, 1, 1))

        for k in range(probes):
            once[k] = operator(prob[k])
        for k in range(probes):
            image[k] = operator(once[k])
            image[k, r_in, c_in] = image[k, r_in, c_in] + own[k * rows:(k + 1) * rows]

        for copy in obs_copies:
            copy.wait_recv()

        def side(n, column, lane):
            text = w_recv[n]
            r, c = text[probes:probes + 1], text[probes + 1:probes + 2]
            hit = jnp.logical_and(c == float(column), iota((PAD_C, slots), 0) == lane)
            in_r = (iota((rows, slots), 0).astype(F32) == r).astype(F32)
            lhs = jnp.concatenate([in_r * text[k:k + 1] for k in range(probes)], axis=0)
            return times(lhs, hit.astype(F32).astype(BF16), NT)

        def end(n, row):
            text = w_recv[n]
            r, c = text[probes:probes + 1], text[probes + 1:probes + 2]
            in_c = (iota((cols, slots), 0).astype(F32) == c).astype(F32).astype(BF16)
            return times(jnp.where(r == float(row), text, 0.0), in_c, NT)

        from_left = side(0, cols - 1, PAD_C - 1)
        from_right = side(1, 0, 0)
        from_above = end(2, rows - 1)
        from_below = end(3, 0)
        for k in range(probes):
            mine = slice(k * rows, (k + 1) * rows)
            image[k, r_in, halo_c[-1]] = image[k, r_in, halo_c[-1]] + from_left[mine]
            image[k, r_in, halo_c[1]] = image[k, r_in, halo_c[1]] + from_right[mine]
            image[k, PAD_R - 1:PAD_R, c_in] = image[k, PAD_R - 1:PAD_R, c_in] + from_above[k:k + 1]
            image[k, PAD_R + rows:PAD_R + rows + 1, c_in] = (
                image[k, PAD_R + rows:PAD_R + rows + 1, c_in] + from_below[k:k + 1])

        def fold(x):
            total = jnp.sum(x.reshape(rows // 8, 8, cols), axis=0)
            total = sum(total[:, n * 128:(n + 1) * 128] for n in range(cols // 128))
            return jnp.sum(total, axis=0, keepdims=True)

        block = jnp.concatenate([image[k, r_in, c_in] for k in range(probes)], axis=0)
        picked = times(block, in_col)
        seen = [jnp.sum(picked[k * rows:(k + 1) * rows] * in_row, axis=0, keepdims=True) for k in range(probes)]
        seen = jnp.concatenate(seen + [jnp.zeros((8 - probes, slots), F32)], axis=0)
        seen = jnp.where(keep, seen, 0.0)
        answer = jnp.dot(seen, weight, precision=lax.Precision.HIGHEST, preferred_element_type=F32)
        quad = seen * answer
        quad = sum(quad[:, n * 128:(n + 1) * 128] for n in range(slots // 128))
        firsts, seconds, thirds = [], [], []
        for k in range(probes):
            field = image[k]
            inner = field[r_in, c_in]
            firsts.append(fold(prob[k, r_in, c_in] * inner))
            seconds.append(fold(inner * inner))
            twice = operator(field)[r_in, c_in]
            thirds.append(fold(twice * twice) + quad[k:k + 1])
        lines = jnp.concatenate(firsts + seconds + thirds + [jnp.zeros((16 - 3 * probes, 128), F32)], axis=0)
        sums = jnp.sum(lines, axis=1, keepdims=True)
        total = jnp.sum(jnp.where(iota((16, 128), 0) == iota((16, 128), 1), sums, 0.0), axis=0, keepdims=True)

        for stage, (size, got, ssem, rsem) in enumerate(((by, got_y, y_send, y_recv), (bx, got_x, x_send, x_recv))):
            part[stage] = total
            copies = []
            for d in range(1, size):
                copy = pltpu.make_async_remote_copy(
                    src_ref=part.at[stage], dst_ref=got.at[d - 1],
                    send_sem=ssem.at[d - 1], recv_sem=rsem.at[d - 1],
                    device_id=at(0, d) if stage == 0 else at(d, 0), device_id_type=MESH)
                copy.start()
                copies.append(copy)
            for d, copy in enumerate(copies):
                copy.wait_recv()
                total = total + got[d]
            sends += copies

        lane = iota((1, 128), 1)
        m1 = jnp.where(lane < probes, total, 1.0)
        m2 = jnp.where(lane < probes, pltpu.roll(total, 128 - probes, 1), 1.0)
        m3 = jnp.where(lane < probes, pltpu.roll(total, 128 - 2 * probes, 1), 1.0)
        norm0 = float(nx * ny)
        alpha0 = norm0 / m1
        norm1 = alpha0 * alpha0 * m2 - norm0
        alpha1 = norm1 / (alpha0 * alpha0 * (m3 - m2 * m2 / m1))
        on_probe = alpha0 + alpha1 * (1.0 + norm1 / norm0)
        on_image = alpha1 * alpha0
        trace = jnp.sum(jnp.where(lane < probes, alpha0 * norm0 + alpha1 * norm1, 0.0)) / probes
        trace_ref[0, 0] = trace
        for k in range(probes):
            sol_ref[k] = on_probe[0, k] * prob[k, r_in, c_in] - on_image[0, k] * image[k, r_in, c_in]
        for copy in sends:
            copy.wait_send()

    return body, ext_r, ext_c


def solution(mesh):
    bx, by = mesh.shape["gx"], mesh.shape["gy"]

    def per_device(probe_seeds, damping, coupling_x, coupling_y, sensor_count, sensor_cells, obs_weight):
        probes = probe_seeds.shape[0]
        rows, cols = damping.shape
        slots = sensor_cells.shape[-1]
        body, ext_r, ext_c = kernel_of(probes, bx, by, rows, cols)
        dma = pltpu.SemaphoreType.DMA
        sol, trace = pl.pallas_call(
            body,
            name="two_steps",
            out_shape=(jax.ShapeDtypeStruct((probes, rows, cols), F32), jax.ShapeDtypeStruct((1, 1), F32)),
            in_specs=[pl.BlockSpec(memory_space=pl.ANY)] * 7,
            out_specs=(pl.BlockSpec(memory_space=pltpu.VMEM), pl.BlockSpec(memory_space=pltpu.SMEM)),
            scratch_shapes=[
                pltpu.SMEM((1, probes), jnp.int32), pltpu.SMEM((1, 1), jnp.int32),
                pltpu.VMEM((1, slots), jnp.int32), pltpu.VMEM((slots, slots), F32),
                pltpu.VMEM((3, ext_r, ext_c), F32),
                pltpu.VMEM((ext_r, ext_c), F32), pltpu.VMEM((ext_r, ext_c), F32), pltpu.VMEM((ext_r, ext_c), F32),
                pltpu.VMEM((probes, ext_r, ext_c), F32), pltpu.VMEM((probes, ext_r, ext_c), F32),
                pltpu.VMEM((probes, ext_r, ext_c), F32),
                pltpu.VMEM((8, slots), F32), pltpu.VMEM((4, 8, slots), F32),
                pltpu.VMEM((2, 1, 128), F32), pltpu.VMEM((by - 1, 1, 128), F32), pltpu.VMEM((bx - 1, 1, 128), F32),
                dma((7,)), dma((8,)), dma((8,)), dma((4,)), dma((4,)),
                dma((by - 1,)), dma((by - 1,)), dma((bx - 1,)), dma((bx - 1,)),
            ],
            compiler_params=pltpu.CompilerParams(collective_id=0, has_side_effects=True),
        )(probe_seeds.reshape(1, probes), damping, coupling_x, coupling_y, sensor_count,
          sensor_cells.reshape(1, slots), obs_weight.reshape(slots, slots))
        return sol, trace.reshape(())

    return jax.shard_map(
        per_device,
        mesh=mesh,
        in_specs=(P(), P("gx", "gy"), P("gx", "gy"), P("gx", "gy"), P("gx", "gy"),
                  P("gx", "gy", None), P("gx", "gy", None, None)),
        out_specs=(P(None, "gx", "gy"), P()),
        check_vma=False,
    )
```

time: 179 us -> 39.5 us (0.22)
  blocking collectives: 65.9 us -> 0 us
  starting transfers between devices: 43 us -> 0 us
  Pallas kernels: 0 us -> 34.5 us
  local copies, waits for them, and re-layouts: 31.6 us -> 1.67 us
  other arithmetic: 19.2 us -> 0 us
  waiting for transfers between devices: 15 us -> 0 us
    all_to_all x5 -> x0, blocking collectives: 65.9 us -> none  [copy_for_each(): lax.all_to_all(jnp.broadcast_to(array[None], (devices, *array.shape)), ax...]
    ppermute x12 -> x0, starting transfers between devices: 38.9 us -> none  [the longest x6 25.1 us: with_halo(): lax.ppermute(head, axis, [((i + 1) % count, i) for i in range(count)])]
    pallas_call x0 -> x1, Pallas kernels: none -> 34.5 us  [per_device(): pl.pallas_call(body, name='two_steps', out_shape=(jax.ShapeDtypeStruct((p...]
    reshape x2 -> x0, local copies, waits for them, and re-layouts: 10.5 us -> none  [observe(): jnp.zeros_like(flat).at[:, cell_ids].add(weighted).reshape(field.shape)]
    scatter-add x2 -> x0, other arithmetic: 10.3 us -> none  [observe(): jnp.zeros_like(flat).at[:, cell_ids].add(weighted).reshape(field.shape)]
    ppermute x12 -> x0, waiting for transfers between devices: 8.48 us -> none  [the longest x6 5.21 us: with_halo(): lax.ppermute(head, axis, [((i + 1) % count, i) for i in range(count)])]
    gather x2 -> x0, local copies, waits for them, and re-layouts: 8.21 us -> none  [observe(): sampled = jnp.take(flat, cell_ids, axis=1) * mask]
    all_to_all x1 -> x0, waiting for transfers between devices: 6.48 us -> none  [copy_for_each(): lax.all_to_all(jnp.broadcast_to(array[None], (devices, *array.shape)), ax...]
  transfers between devices with their start and end apart: 13 -> 0, of which waited for: 5 -> 0; matrix products, arithmetic and copies ran while one was open for 21% -> 0% of each run, Pallas kernels for 0% -> 0%
where the time goes in v1:
time: 39.5 us; the launch traced here: 39.2 us
  Pallas kernels  34.5 us (87%)
  between operations  3.05 us (8%)
  local copies, waits for them, and re-layouts  1.67 us (4%)
    pallas_call x1, Pallas kernels, per_device(): pl.pallas_call(body, name='two_steps', out_shape=(jax.ShapeDtypeStruct((p...  34.5 us
    unnamed x1, local copies, waits for them, and re-layouts  1.67 us

profile of v1, /device:TPU:1, one launch (start us, length us, event | category | flops | bytes accessed | tf_op | source)
XLA Modules:
  0.0 39.2 jit_solution(8467019158603076592)
XLA Ops:
  1.3 34.5 %two_steps.1 = (f32[4,64,256]{2,1,0:T(8,128)}, f32[1,1]{1,0:T(1,128)}) custom-call(s32[1,4]{1,0:T(1,128)} %bitcast.6, f32[64,256]{1,0:T(8,128)} %damp_h.1, f32[64,256]{1,0:T(8,128)} %cx_h.1, f32[64,256]{1,0:T(8,128)} %cy_h.1, s32[1,1]{1,0:T(1,128)S(6)} %copy.11.count_h, s32[1,256]{1,0:T(1,128)} %bitcast.5, f32[256,256]{1,0:T(8,128)} %bitcast.4), custom_call_target="tpu_custom_call" | custom-call | tf_op jit(solution)/shard_map/two_steps/pallas_call | solution.py:264
  35.8 1.7 %copy.12 = f32[4,64,256]{2,1,0:T(8,128)} copy(f32[4,64,256]{2,1,0:T(8,128)} %get-tuple-element.8) | data formatting | bytes 524288

commit v2 on v1

v2 whole, which is shorter than its diff:
```python
import jax
import jax.numpy as jnp
from jax import lax
from jax.experimental import pallas as pl
from jax.experimental.pallas import tpu as pltpu
from jax.sharding import PartitionSpec as P

MESH = pl.DeviceIdType.MESH
NT = (((1,), (1,)), ((), ()))
F32 = jnp.float32
BF16 = jnp.bfloat16

PAD_R, PAD_C = 8, 128
GROUP = 16


def mix(base):
    mixed = (base ^ ((base >> 16) & 65535)) * 73244475
    mixed = (mixed ^ ((mixed >> 16) & 65535)) * 73244475
    mixed = mixed ^ ((mixed >> 16) & 65535)
    return (2 * ((mixed >> 7) & 1) - 1).astype(F32)


def position(rows, cols):
    return rows * 374761393 + cols * 1103515245


def iota(shape, dim):
    return lax.broadcasted_iota(jnp.int32, shape, dim)


def split3(x):
    high = x.astype(BF16)
    rest = x - high.astype(F32)
    mid = rest.astype(BF16)
    low = (rest - mid.astype(F32)).astype(BF16)
    return high, mid, low


def times(x, y, dims=(((1,), (0,)), ((), ()))):
    total = None
    for part in reversed(split3(x)):
        one = lax.dot_general(part, y, dims, preferred_element_type=F32)
        total = one if total is None else total + one
    return total


def hbm(x):
    return pltpu.with_memory_space_constraint(x, pltpu.HBM)


def kernel_of(probes, bx, by, rows, cols):
    ext_r, ext_c = rows + PAD_R, cols + PAD_C
    nx, ny = bx * rows, by * cols
    r_in, c_in = slice(0, rows), slice(0, cols)
    r_out, c_out = slice(rows, ext_r), slice(cols, ext_c)
    tiles = rows // 8
    cross = [(0, 1), (0, -1), (1, 0), (-1, 0)]
    corners = [(a, b) for a in (-1, 1) for b in (-1, 1)]

    def body(seeds_h, damp_h, cx_h, cy_h, count_s, cells_h, weight_h, image_h, prob_h, total_ref,
             seeds_s, cells_v, weight_v, coef, up_v, left_v, diag_v, prob, once, image, inner_v,
             edge_v, col_send, row_recv, col_recv, diag_recv, w_send, w_recv, part, got_y, got_x,
             local_sem, coef_send, coef_recv, obs_send, obs_recv, y_send, y_recv, x_send, x_recv):
        gx, gy = lax.axis_index("gx"), lax.axis_index("gy")

        def at(dx, dy):
            return (lax.rem(gx + (dx + bx), bx), lax.rem(gy + (dy + by), by))

        barrier = pltpu.get_barrier_semaphore()
        nearest = [(0, 1), (0, by - 1), (1, 0), (bx - 1, 0)] + corners
        peers = nearest + [(0, d) for d in range(2, by - 1)] + [(d, 0) for d in range(2, bx - 1)]
        for dx, dy in peers:
            pl.semaphore_signal(barrier, inc=1, device_id=at(dx, dy), device_id_type=MESH)

        loads = [
            pltpu.make_async_copy(damp_h, coef.at[0, r_in, c_in], local_sem.at[0]),
            pltpu.make_async_copy(cx_h, coef.at[1, r_in, c_in], local_sem.at[1]),
            pltpu.make_async_copy(cy_h, coef.at[2, r_in, c_in], local_sem.at[2]),
            pltpu.make_async_copy(cells_h, cells_v, local_sem.at[3]),
            pltpu.make_async_copy(seeds_h, seeds_s, local_sem.at[4]),
            pltpu.make_async_copy(weight_h, weight_v, local_sem.at[5]),
        ]
        for load in loads:
            load.start()
        for load in loads[:3]:
            load.wait()

        lane = iota((rows, 128), 1)
        for n, (start, base) in enumerate(((cols - 128, 3), (0, 0))):
            d, x, y = (coef[i, r_in, start:start + 128] for i in range(3))
            d = pltpu.roll(d, base, 1) if base else d
            edge = jnp.where(lane < 3, d, jnp.where(lane < 6, pltpu.roll(x, base + 3, 1), pltpu.roll(y, base + 6, 1)))
            edge_v[n] = edge
            tile = edge[0:8]
            for a in range(1, tiles):
                tile = jnp.where(lane[0:8] < a * GROUP, tile, pltpu.roll(edge[8 * a:8 * a + 8], a * GROUP, 1))
            col_send[n] = tile
        pl.semaphore_wait(barrier, len(peers))

        sends = []

        def send(src, dst, ssem, rsem, dx, dy):
            copy = pltpu.make_async_remote_copy(
                src_ref=src, dst_ref=dst, send_sem=ssem, recv_sem=rsem,
                device_id=at(dx, dy), device_id_type=MESH)
            copy.start()
            sends.append(copy)
            return copy

        coef_copies = [
            send(col_send.at[n], col_recv.at[n], coef_send.at[n], coef_recv.at[n], 0, 1 - 2 * n) for n in range(2)
        ] + [
            send(coef.at[:, rows - 8:rows, c_in] if n == 0 else coef.at[:, 0:8, c_in], row_recv.at[n],
                 coef_send.at[2 + n], coef_recv.at[2 + n], 1 - 2 * n, 0) for n in range(2)
        ] + [
            send(edge_v.at[m, rows - 8:rows] if n == 0 else edge_v.at[m, 0:8], diag_recv.at[n, m],
                 coef_send.at[4 + 2 * n + m], coef_recv.at[4 + 2 * n + m], 1 - 2 * n, 1 - 2 * m)
            for n in range(2) for m in range(2)
        ]

        for load in loads[3:5]:
            load.wait()
        slots = cells_v.shape[1]
        cell = cells_v[...]
        sensor_r = lax.div(cell, cols)
        sensor_c = lax.rem(cell, cols)
        sub = iota((8, slots), 0)
        seed = jnp.where(sub == 0, seeds_s[0, 0], 0)
        for k in range(1, probes):
            seed = jnp.where(sub == k, seeds_s[0, k], seed)
        live = iota((8, slots), 1) < count_s[0, 0]
        keep = jnp.logical_and(live, sub < probes)
        sampled = mix(seed * 668265261 + position(gx * rows + sensor_r, gy * cols + sensor_c))
        sampled = jnp.where(keep, sampled, 0.0)
        loads[5].wait()
        weight = weight_v[...]
        weighted = jnp.dot(sampled, weight, precision=lax.Precision.HIGHEST, preferred_element_type=F32)
        weighted = jnp.where(keep, weighted, 0.0)
        row_f, col_f = sensor_r.astype(F32), sensor_c.astype(F32)
        message = jnp.where(sub == probes, jnp.broadcast_to(row_f, (8, slots)), weighted)
        message = jnp.where(sub == probes + 1, jnp.broadcast_to(col_f, (8, slots)), message)
        w_send[...] = message
        obs_copies = [
            send(w_send, w_recv.at[n], obs_send.at[n], obs_recv.at[n], dx, dy) for n, (dx, dy) in enumerate(cross)
        ]

        row_ids, col_ids = iota((ext_r, ext_c), 0), iota((ext_r, ext_c), 1)
        row_ids = jnp.where(row_ids < rows + PAD_R // 2, row_ids, row_ids - ext_r)
        col_ids = jnp.where(col_ids < cols + PAD_C // 2, col_ids, col_ids - ext_c)
        place = position((gx * rows + row_ids) & (nx - 1), (gy * cols + col_ids) & (ny - 1))
        for k in range(probes):
            prob[k] = mix(seeds_s[0, k] * 668265261 + place)
        saves = [pltpu.make_async_copy(prob.at[:, r_in, c_in], prob_h, local_sem.at[6])]
        saves[0].start()

        in_row = (iota((rows, slots), 0) == sensor_r).astype(F32)
        in_col = (iota((cols, slots), 0) == sensor_c).astype(F32).astype(BF16)
        spread = jnp.concatenate([in_row * weighted[k:k + 1] for k in range(probes)], axis=0)
        own = times(spread, in_col, NT)

        for copy in coef_copies:
            copy.wait_recv()
        right = lane[0:8] < 64
        below = iota((8, 128), 0) < 4
        from_left, from_right = col_recv[0], col_recv[1]
        for i in range(3):
            for a in range(tiles):
                coef[i, 8 * a:8 * a + 8, c_out] = jnp.where(
                    right, pltpu.roll(from_right, (256 - 3 * i - a * GROUP) % 128, 1),
                    pltpu.roll(from_left, (256 + 125 - 3 * i - a * GROUP) % 128, 1))
            coef[i, r_out, c_in] = jnp.where(iota((8, cols), 0) < 4, row_recv[1, i], row_recv[0, i])
            corner = [[pltpu.roll(diag_recv[n, m], (256 + 125 * (1 - m) - 3 * i) % 128, 1) for m in range(2)]
                      for n in range(2)]
            coef[i, r_out, c_out] = jnp.where(
                below, jnp.where(right, corner[1][1], corner[1][0]), jnp.where(right, corner[0][1], corner[0][0]))
        damp, cx, cy = coef[0], coef[1], coef[2]
        cxu, cyl = pltpu.roll(cx, 1, 0), pltpu.roll(cy, 1, 1)
        up_v[...] = cxu
        left_v[...] = cyl
        diag_v[...] = damp + cx + cxu + cy + cyl

        def operator(field):
            return (diag_v[...] * field - coef[1] * pltpu.roll(field, ext_r - 1, 0) - up_v[...] * pltpu.roll(field, 1, 0)
                    - coef[2] * pltpu.roll(field, ext_c - 1, 1) - left_v[...] * pltpu.roll(field, 1, 1))

        for k in range(probes):
            once[k] = operator(prob[k])

        for copy in obs_copies:
            copy.wait_recv()

        def side(n, column, at_lane):
            text = w_recv[n]
            r, c = text[probes:probes + 1], text[probes + 1:probes + 2]
            hit = jnp.logical_and(c == float(column), iota((PAD_C, slots), 0) == at_lane)
            in_r = (iota((rows, slots), 0).astype(F32) == r).astype(F32)
            lhs = jnp.concatenate([in_r * text[k:k + 1] for k in range(probes)], axis=0)
            return times(lhs, hit.astype(F32).astype(BF16), NT)

        def end(n, row):
            text = w_recv[n]
            r, c = text[probes:probes + 1], text[probes + 1:probes + 2]
            in_c = (iota((cols, slots), 0).astype(F32) == c).astype(F32).astype(BF16)
            return times(jnp.where(r == float(row), text, 0.0), in_c, NT)

        beside = side(0, cols - 1, PAD_C - 1) + side(1, 0, 0)
        above_obs = end(2, rows - 1)
        below_obs = end(3, 0)
        for k in range(probes):
            mine = slice(k * rows, (k + 1) * rows)
            image[k] = operator(once[k])
            inner = image[k, r_in, c_in] + own[mine]
            image[k, r_in, c_in] = inner
            inner_v[k] = inner
            image[k, r_in, c_out] = image[k, r_in, c_out] + beside[mine]
            image[k, ext_r - 1:ext_r, c_in] = image[k, ext_r - 1:ext_r, c_in] + above_obs[k:k + 1]
            image[k, rows:rows + 1, c_in] = image[k, rows:rows + 1, c_in] + below_obs[k:k + 1]
        saves.append(pltpu.make_async_copy(inner_v, image_h, local_sem.at[7]))
        saves[1].start()

        def fold(x):
            total = jnp.sum(x.reshape(rows // 8, 8, cols), axis=0)
            total = sum(total[:, n * 128:(n + 1) * 128] for n in range(cols // 128))
            return jnp.sum(total, axis=0, keepdims=True)

        block = jnp.concatenate([image[k, r_in, c_in] for k in range(probes)], axis=0)
        picked = times(block, in_col)
        seen = [jnp.sum(picked[k * rows:(k + 1) * rows] * in_row, axis=0, keepdims=True) for k in range(probes)]
        seen = jnp.concatenate(seen + [jnp.zeros((8 - probes, slots), F32)], axis=0)
        seen = jnp.where(keep, seen, 0.0)
        answer = jnp.dot(seen, weight, precision=lax.Precision.HIGHEST, preferred_element_type=F32)
        quad = seen * answer
        quad = sum(quad[:, n * 128:(n + 1) * 128] for n in range(slots // 128))
        firsts, seconds, thirds = [], [], []
        for k in range(probes):
            field = image[k]
            inner = field[r_in, c_in]
            firsts.append(fold(prob[k, r_in, c_in] * inner))
            seconds.append(fold(inner * inner))
            twice = operator(field)[r_in, c_in]
            thirds.append(fold(twice * twice) + quad[k:k + 1])
        lines = jnp.concatenate(firsts + seconds + thirds + [jnp.zeros((16 - 3 * probes, 128), F32)], axis=0)
        sums = jnp.sum(lines, axis=1, keepdims=True)
        total = jnp.sum(jnp.where(iota((16, 128), 0) == iota((16, 128), 1), sums, 0.0), axis=0, keepdims=True)

        for stage, (size, got, ssem, rsem) in enumerate(((by, got_y, y_send, y_recv), (bx, got_x, x_send, x_recv))):
            part[stage] = total
            copies = [
                send(part.at[stage], got.at[d - 1], ssem.at[d - 1], rsem.at[d - 1], *((0, d) if stage == 0 else (d, 0)))
                for d in range(1, size)
            ]
            for d, copy in enumerate(copies):
                copy.wait_recv()
                total = total + got[d]
        total_ref[...] = total
        for save in saves:
            save.wait()
        for copy in sends:
            copy.wait_send()

    def finish(total_ref, image_ref, prob_ref, sol_ref, trace_ref):
        total = total_ref[...]
        lane = iota((1, 128), 1)
        m1 = jnp.where(lane < probes, total, 1.0)
        m2 = jnp.where(lane < probes, pltpu.roll(total, 128 - probes, 1), 1.0)
        m3 = jnp.where(lane < probes, pltpu.roll(total, 128 - 2 * probes, 1), 1.0)
        norm0 = float(nx * ny)
        alpha0 = norm0 / m1
        norm1 = alpha0 * alpha0 * m2 - norm0
        alpha1 = norm1 / (alpha0 * alpha0 * (m3 - m2 * m2 / m1))
        on_probe = alpha0 + alpha1 * (1.0 + norm1 / norm0)
        on_image = alpha1 * alpha0
        trace_ref[0, 0] = jnp.sum(jnp.where(lane < probes, alpha0 * norm0 + alpha1 * norm1, 0.0)) / probes
        for k in range(probes):
            sol_ref[k] = on_probe[0, k] * prob_ref[k] - on_image[0, k] * image_ref[k]

    return body, finish, ext_r, ext_c


def solution(mesh):
    bx, by = mesh.shape["gx"], mesh.shape["gy"]

    def per_device(probe_seeds, damping, coupling_x, coupling_y, sensor_count, sensor_cells, obs_weight):
        probes = probe_seeds.shape[0]
        rows, cols = damping.shape
        slots = sensor_cells.shape[-1]
        body, finish, ext_r, ext_c = kernel_of(probes, bx, by, rows, cols)
        dma = pltpu.SemaphoreType.DMA
        plane = pltpu.VMEM((ext_r, ext_c), F32)
        fields = pltpu.VMEM((probes, ext_r, ext_c), F32)
        in_vmem = pl.BlockSpec(memory_space=pltpu.VMEM)
        in_hbm = pl.BlockSpec(memory_space=pltpu.HBM)
        in_smem = pl.BlockSpec(memory_space=pltpu.SMEM)
        field = jax.ShapeDtypeStruct((probes, rows, cols), F32)
        image, prob, total = pl.pallas_call(
            body,
            name="two_steps",
            out_shape=(field, field, jax.ShapeDtypeStruct((1, 128), F32)),
            in_specs=[in_hbm] * 4 + [in_smem] + [in_hbm] * 2,
            out_specs=(pl.BlockSpec(memory_space=pl.ANY), pl.BlockSpec(memory_space=pl.ANY), in_vmem),
            scratch_shapes=[
                pltpu.SMEM((1, probes), jnp.int32),
                pltpu.VMEM((1, slots), jnp.int32), pltpu.VMEM((slots, slots), F32),
                pltpu.VMEM((3, ext_r, ext_c), F32), plane, plane, plane, fields, fields, fields,
                pltpu.VMEM((probes, rows, cols), F32),
                pltpu.VMEM((2, rows, 128), F32), pltpu.VMEM((2, 8, 128), F32),
                pltpu.VMEM((2, 3, 8, cols), F32), pltpu.VMEM((2, 8, 128), F32), pltpu.VMEM((2, 2, 8, 128), F32),
                pltpu.VMEM((8, slots), F32), pltpu.VMEM((4, 8, slots), F32),
                pltpu.VMEM((2, 1, 128), F32), pltpu.VMEM((by - 1, 1, 128), F32), pltpu.VMEM((bx - 1, 1, 128), F32),
                dma((8,)), dma((8,)), dma((8,)), dma((4,)), dma((4,)),
                dma((by - 1,)), dma((by - 1,)), dma((bx - 1,)), dma((bx - 1,)),
            ],
            compiler_params=pltpu.CompilerParams(
                collective_id=0, has_side_effects=True, vmem_limit_bytes=16 * 2**20),
        )(hbm(probe_seeds.reshape(1, probes)), hbm(damping), hbm(coupling_x), hbm(coupling_y), sensor_count,
          hbm(sensor_cells.reshape(1, slots)), hbm(obs_weight.reshape(slots, slots)))
        sol, trace = pl.pallas_call(
            finish,
            name="finish",
            out_shape=(field, jax.ShapeDtypeStruct((1, 1), F32)),
            in_specs=[in_vmem] * 3,
            out_specs=(in_vmem, in_smem),
            compiler_params=pltpu.CompilerParams(vmem_limit_bytes=16 * 2**20),
        )(total, image, prob)
        return sol, trace.reshape(())

    return jax.shard_map(
        per_device,
        mesh=mesh,
        in_specs=(P(), P("gx", "gy"), P("gx", "gy"), P("gx", "gy"), P("gx", "gy"),
                  P("gx", "gy", None), P("gx", "gy", None, None)),
        out_specs=(P(None, "gx", "gy"), P()),
        check_vma=False,
    )
```

time: 39.5 us -> 35.6 us (0.901)
  between operations: 3.05 us -> 1.29 us
  local copies, waits for them, and re-layouts: 1.67 us -> 0 us
  Pallas kernels: 34.5 us -> 34.1 us
    unnamed x1 -> x0, local copies, waits for them, and re-layouts: 1.67 us -> none
    pallas_call x1 -> x2, Pallas kernels: 34.5 us -> 34.1 us  [the longest x1 33.2 us: per_device(): pl.pallas_call(body, name='two_steps', out_shape=(field, field, jax.Shape...]
where the time goes in v2:
time: 35.6 us; the launch traced here: 35.4 us
  Pallas kernels  34.1 us (96%)
  between operations  1.29 us (4%)
    pallas_call x1, Pallas kernels, per_device(): pl.pallas_call(body, name='two_steps', out_shape=(field, field, jax.Shape...  33.2 us
    pallas_call x1, Pallas kernels, per_device(): pl.pallas_call(finish, name='finish', out_shape=(field, jax.ShapeDtypeStr...  0.96 us

profile of v2, /device:TPU:1, one launch (start us, length us, event | category | flops | bytes accessed | tf_op | source)
XLA Modules:
  0.0 35.4 jit_solution(5448822553074532787)
XLA Ops:
  1.3 33.2 %two_steps.1 = (f32[4,64,256]{2,1,0:T(8,128)S(1)}, f32[4,64,256]{2,1,0:T(8,128)S(1)}, f32[1,128]{1,0:T(1,128)S(1)}) custom-call(s32[1,4]{1,0:T(1,128)} %bitcast.6, f32[64,256]{1,0:T(8,128)} %damp_h.1, f32[64,256]{1,0:T(8,128)} %cx_h.1, f32[64,256]{1,0:T(8,128)} %cy_h.1, s32[1,1]{1,0:T(1,128)S(6)} %copy.9.count_s, s32[1,256]{1,0:T(1,128)} %bitcast.5, ...), custom_call_target="tpu_custom_call" | custom-call | tf_op jit(solution)/shard_map/two_steps/pallas_call | solution.py:296
  34.4 1.0 %finish.1 = (f32[4,64,256]{2,1,0:T(8,128)}, f32[1,1]{1,0:T(1,128)}) custom-call(f32[1,128]{1,0:T(1,128)S(1)} %get-tuple-element.7.total_ref, f32[4,64,256]{2,1,0:T(8,128)S(1)} %get-tuple-element.8.image_ref, f32[4,64,256]{2,1,0:T(8,128)S(1)} %get-tuple-element.9.prob_ref), custom_call_target="tpu_custom_call" | custom-call | tf_op jit(solution)/shard_map/finish/pallas_call | solution.py:318

commit v3 on v2

--- a/solution.py
+++ b/solution.py
@@ -60,8 +60,8 @@
 
     def body(seeds_h, damp_h, cx_h, cy_h, count_s, cells_h, weight_h, image_h, prob_h, total_ref,
              seeds_s, cells_v, weight_v, coef, up_v, left_v, diag_v, prob, once, image, inner_v,
-             edge_v, col_send, row_recv, col_recv, diag_recv, w_send, w_recv, part, got_y, got_x,
-             local_sem, coef_send, coef_recv, obs_send, obs_recv, y_send, y_recv, x_send, x_recv):
+             edge_v, col_send, row_send, row_recv, col_recv, diag_recv, w_send, w_recv, part, got_y, got_x,
+             local_sem, known_sem, coef_send, coef_recv, obs_send, obs_recv, y_send, y_recv, x_send, x_recv):
         gx, gy = lax.axis_index("gx"), lax.axis_index("gy")
 
         def at(dx, dy):
@@ -69,8 +69,7 @@
 
         barrier = pltpu.get_barrier_semaphore()
         nearest = [(0, 1), (0, by - 1), (1, 0), (bx - 1, 0)] + corners
-        peers = nearest + [(0, d) for d in range(2, by - 1)] + [(d, 0) for d in range(2, bx - 1)]
-        for dx, dy in peers:
+        for dx, dy in nearest:
             pl.semaphore_signal(barrier, inc=1, device_id=at(dx, dy), device_id_type=MESH)
 
         loads = [
@@ -96,29 +95,11 @@
             for a in range(1, tiles):
                 tile = jnp.where(lane[0:8] < a * GROUP, tile, pltpu.roll(edge[8 * a:8 * a + 8], a * GROUP, 1))
             col_send[n] = tile
-        pl.semaphore_wait(barrier, len(peers))
-
-        sends = []
-
-        def send(src, dst, ssem, rsem, dx, dy):
-            copy = pltpu.make_async_remote_copy(
-                src_ref=src, dst_ref=dst, send_sem=ssem, recv_sem=rsem,
-                device_id=at(dx, dy), device_id_type=MESH)
-            copy.start()
-            sends.append(copy)
-            return copy
-
-        coef_copies = [
-            send(col_send.at[n], col_recv.at[n], coef_send.at[n], coef_recv.at[n], 0, 1 - 2 * n) for n in range(2)
-        ] + [
-            send(coef.at[:, rows - 8:rows, c_in] if n == 0 else coef.at[:, 0:8, c_in], row_recv.at[n],
-                 coef_send.at[2 + n], coef_recv.at[2 + n], 1 - 2 * n, 0) for n in range(2)
-        ] + [
-            send(edge_v.at[m, rows - 8:rows] if n == 0 else edge_v.at[m, 0:8], diag_recv.at[n, m],
-                 coef_send.at[4 + 2 * n + m], coef_recv.at[4 + 2 * n + m], 1 - 2 * n, 1 - 2 * m)
-            for n in range(2) for m in range(2)
-        ]
-
+        for n, base in enumerate((rows - 3, 0)):
+            row_send[n, 0:2] = coef[0, base + 1 - n:base + 3 - n, c_in]
+            row_send[n, 2:5] = coef[1, base:base + 3, c_in]
+            row_send[n, 5:7] = coef[2, base + 1 - n:base + 3 - n, c_in]
+            row_send[n, 7:8] = coef[2, base:base + 1, c_in]
         for load in loads[3:5]:
             load.wait()
         slots = cells_v.shape[1]
@@ -134,13 +115,63 @@
         sampled = mix(seed * 668265261 + position(gx * rows + sensor_r, gy * cols + sensor_c))
         sampled = jnp.where(keep, sampled, 0.0)
         loads[5].wait()
-        weight = weight_v[...]
-        weighted = jnp.dot(sampled, weight, precision=lax.Precision.HIGHEST, preferred_element_type=F32)
+        weight = split3(weight_v[...])
+
+        def weigh(x):
+            high, mid, low = split3(x)
+            parts = (jnp.concatenate([high, mid, low], axis=0), jnp.concatenate([high, mid], axis=0), high)
+            done = [jnp.dot(x_part, w_part, preferred_element_type=F32) for x_part, w_part in zip(parts, weight)]
+            return ((done[0][16:24] + done[1][8:16] + done[2]) + (done[0][8:16] + done[1][0:8])) + done[0][0:8]
+
+        exact = sampled.astype(BF16)
+        weighted = sum(jnp.dot(exact, part, preferred_element_type=F32) for part in reversed(weight))
         weighted = jnp.where(keep, weighted, 0.0)
         row_f, col_f = sensor_r.astype(F32), sensor_c.astype(F32)
         message = jnp.where(sub == probes, jnp.broadcast_to(row_f, (8, slots)), weighted)
         message = jnp.where(sub == probes + 1, jnp.broadcast_to(col_f, (8, slots)), message)
         w_send[...] = message
+
+        pl.semaphore_wait(barrier, len(nearest))
+
+        assert (bx, by) == (32, 16)
+
+        def hail(axis, step):
+            for m, d in enumerate((2**step, -2**step)):
+                pl.semaphore_signal(known_sem.at[axis, step, m], inc=1, device_id=at(*((d, 0), (0, d))[axis]),
+                                    device_id_type=MESH)
+
+        def heard(axis, step):
+            for m in range(2):
+                pl.semaphore_wait(known_sem.at[axis, step, m], 1)
+
+        def relay(axis, step):
+            heard(axis, step)
+            hail(axis, step + 1)
+
+        hail(0, 0)
+        hail(1, 0)
+
+        sends = []
+
+        def send(src, dst, ssem, rsem, dx, dy):
+            copy = pltpu.make_async_remote_copy(
+                src_ref=src, dst_ref=dst, send_sem=ssem, recv_sem=rsem,
+                device_id=at(dx, dy), device_id_type=MESH)
+            copy.start()
+            sends.append(copy)
+            return copy
+
+        coef_copies = [
+            send(edge_v.at[m, rows - 8:rows] if n == 0 else edge_v.at[m, 0:8], diag_recv.at[n, m],
+                 coef_send.at[4 + 2 * n + m], coef_recv.at[4 + 2 * n + m], 1 - 2 * n, 1 - 2 * m)
+            for n in range(2) for m in range(2)
+        ] + [
+            send(row_send.at[n], row_recv.at[n], coef_send.at[2 + n], coef_recv.at[2 + n], 1 - 2 * n, 0)
+            for n in range(2)
+        ] + [
+            send(col_send.at[n], col_recv.at[n], coef_send.at[n], coef_recv.at[n], 0, 1 - 2 * n) for n in range(2)
+        ]
+
         obs_copies = [
             send(w_send, w_recv.at[n], obs_send.at[n], obs_recv.at[n], dx, dy) for n, (dx, dy) in enumerate(cross)
         ]
@@ -158,6 +189,33 @@
         in_col = (iota((cols, slots), 0) == sensor_c).astype(F32).astype(BF16)
         spread = jnp.concatenate([in_row * weighted[k:k + 1] for k in range(probes)], axis=0)
         own = times(spread, in_col, NT)
+
+        relay(1, 0)
+        relay(0, 0)
+
+        for copy in obs_copies:
+            copy.wait_recv()
+
+        def side(n, column, at_lane):
+            text = w_recv[n]
+            r, c = text[probes:probes + 1], text[probes + 1:probes + 2]
+            hit = jnp.logical_and(c == float(column), iota((PAD_C, slots), 0) == at_lane)
+            in_r = (iota((rows, slots), 0).astype(F32) == r).astype(F32)
+            lhs = jnp.concatenate([in_r * text[k:k + 1] for k in range(probes)], axis=0)
+            return times(lhs, hit.astype(F32).astype(BF16), NT)
+
+        def end(n, row):
+            text = w_recv[n]
+            r, c = text[probes:probes + 1], text[probes + 1:probes + 2]
+            in_c = (iota((cols, slots), 0).astype(F32) == c).astype(F32).astype(BF16)
+            return times(jnp.where(r == float(row), text, 0.0), in_c, NT)
+
+        beside = side(0, cols - 1, PAD_C - 1) + side(1, 0, 0)
+        above_obs = end(2, rows - 1)
+        below_obs = end(3, 0)
+
+        relay(1, 1)
+        relay(0, 1)
 
         for copy in coef_copies:
             copy.wait_recv()
@@ -169,7 +227,10 @@
                 coef[i, 8 * a:8 * a + 8, c_out] = jnp.where(
                     right, pltpu.roll(from_right, (256 - 3 * i - a * GROUP) % 128, 1),
                     pltpu.roll(from_left, (256 + 125 - 3 * i - a * GROUP) % 128, 1))
-            coef[i, r_out, c_in] = jnp.where(iota((8, cols), 0) < 4, row_recv[1, i], row_recv[0, i])
+            top, bottom = row_recv[1], row_recv[0]
+            first, second = (0, 2, 5)[i], (0, 2, 5)[i] + (2, 3, 2)[i]
+            top, bottom = (pltpu.roll(t, s % 8, 0) if s % 8 else t for t, s in ((top, 8 - first), (bottom, 8 - second)))
+            coef[i, r_out, c_in] = jnp.where(iota((8, cols), 0) < 4, top, bottom)
             corner = [[pltpu.roll(diag_recv[n, m], (256 + 125 * (1 - m) - 3 * i) % 128, 1) for m in range(2)]
                       for n in range(2)]
             coef[i, r_out, c_out] = jnp.where(
@@ -187,26 +248,6 @@
         for k in range(probes):
             once[k] = operator(prob[k])
 
-        for copy in obs_copies:
-            copy.wait_recv()
-
-        def side(n, column, at_lane):
-            text = w_recv[n]
-            r, c = text[probes:probes + 1], text[probes + 1:probes + 2]
-            hit = jnp.logical_and(c == float(column), iota((PAD_C, slots), 0) == at_lane)
-            in_r = (iota((rows, slots), 0).astype(F32) == r).astype(F32)
-            lhs = jnp.concatenate([in_r * text[k:k + 1] for k in range(probes)], axis=0)
-            return times(lhs, hit.astype(F32).astype(BF16), NT)
-
-        def end(n, row):
-            text = w_recv[n]
-            r, c = text[probes:probes + 1], text[probes + 1:probes + 2]
-            in_c = (iota((cols, slots), 0).astype(F32) == c).astype(F32).astype(BF16)
-            return times(jnp.where(r == float(row), text, 0.0), in_c, NT)
-
-        beside = side(0, cols - 1, PAD_C - 1) + side(1, 0, 0)
-        above_obs = end(2, rows - 1)
-        below_obs = end(3, 0)
         for k in range(probes):
             mine = slice(k * rows, (k + 1) * rows)
             image[k] = operator(once[k])
@@ -219,6 +260,8 @@
         saves.append(pltpu.make_async_copy(inner_v, image_h, local_sem.at[7]))
         saves[1].start()
 
+        relay(0, 2)
+
         def fold(x):
             total = jnp.sum(x.reshape(rows // 8, 8, cols), axis=0)
             total = sum(total[:, n * 128:(n + 1) * 128] for n in range(cols // 128))
@@ -229,7 +272,7 @@
         seen = [jnp.sum(picked[k * rows:(k + 1) * rows] * in_row, axis=0, keepdims=True) for k in range(probes)]
         seen = jnp.concatenate(seen + [jnp.zeros((8 - probes, slots), F32)], axis=0)
         seen = jnp.where(keep, seen, 0.0)
-        answer = jnp.dot(seen, weight, precision=lax.Precision.HIGHEST, preferred_element_type=F32)
+        answer = weigh(seen)
         quad = seen * answer
         quad = sum(quad[:, n * 128:(n + 1) * 128] for n in range(slots // 128))
         firsts, seconds, thirds = [], [], []
@@ -245,6 +288,7 @@
         total = jnp.sum(jnp.where(iota((16, 128), 0) == iota((16, 128), 1), sums, 0.0), axis=0, keepdims=True)
 
         for stage, (size, got, ssem, rsem) in enumerate(((by, got_y, y_send, y_recv), (bx, got_x, x_send, x_recv))):
+            heard(1 - stage, 2 + stage)
             part[stage] = total
             copies = [
                 send(part.at[stage], got.at[d - 1], ssem.at[d - 1], rsem.at[d - 1], *((0, d) if stage == 0 else (d, 0)))
@@ -305,10 +349,10 @@
                 pltpu.VMEM((3, ext_r, ext_c), F32), plane, plane, plane, fields, fields, fields,
                 pltpu.VMEM((probes, rows, cols), F32),
                 pltpu.VMEM((2, rows, 128), F32), pltpu.VMEM((2, 8, 128), F32),
-                pltpu.VMEM((2, 3, 8, cols), F32), pltpu.VMEM((2, 8, 128), F32), pltpu.VMEM((2, 2, 8, 128), F32),
+                pltpu.VMEM((2, 8, cols), F32), pltpu.VMEM((2, 8, cols), F32), pltpu.VMEM((2, 8, 128), F32), pltpu.VMEM((2, 2, 8, 128), F32),
                 pltpu.VMEM((8, slots), F32), pltpu.VMEM((4, 8, slots), F32),
                 pltpu.VMEM((2, 1, 128), F32), pltpu.VMEM((by - 1, 1, 128), F32), pltpu.VMEM((bx - 1, 1, 128), F32),
-                dma((8,)), dma((8,)), dma((8,)), dma((4,)), dma((4,)),
+                dma((8,)), pltpu.SemaphoreType.REGULAR((2, 4, 2)), dma((8,)), dma((8,)), dma((4,)), dma((4,)),
                 dma((by - 1,)), dma((by - 1,)), dma((bx - 1,)), dma((bx - 1,)),
             ],
             compiler_params=pltpu.CompilerParams(

time: 35.6 us -> 34.9 us (0.980)
  Pallas kernels: 34.1 us -> 33.4 us
    pallas_call x1, Pallas kernels: 33.2 us -> 32.5 us  [per_device(): pl.pallas_call(body, name='two_steps', out_shape=(field, field, jax.Shape...]
where the time goes in v3:
time: 34.9 us; the launch traced here: 34.7 us
  Pallas kernels  33.4 us (96%)
  between operations  1.29 us (4%)
    pallas_call x1, Pallas kernels, per_device(): pl.pallas_call(body, name='two_steps', out_shape=(field, field, jax.Shape...  32.5 us
    pallas_call x1, Pallas kernels, per_device(): pl.pallas_call(finish, name='finish', out_shape=(field, jax.ShapeDtypeStr...  0.96 us

profile of v3, /device:TPU:1, one launch (start us, length us, event | category | flops | bytes accessed | tf_op | source)
XLA Modules:
  0.0 34.7 jit_solution(11943961965014748136)
XLA Ops:
  1.3 32.5 %two_steps.1 = (f32[4,64,256]{2,1,0:T(8,128)S(1)}, f32[4,64,256]{2,1,0:T(8,128)S(1)}, f32[1,128]{1,0:T(1,128)S(1)}) custom-call(s32[1,4]{1,0:T(1,128)} %bitcast.6, f32[64,256]{1,0:T(8,128)} %damp_h.1, f32[64,256]{1,0:T(8,128)} %cx_h.1, f32[64,256]{1,0:T(8,128)} %cy_h.1, s32[1,1]{1,0:T(1,128)S(6)} %copy.9.count_s, s32[1,256]{1,0:T(1,128)} %bitcast.5, ...), custom_call_target="tpu_custom_call" | custom-call | tf_op jit(solution)/shard_map/two_steps/pallas_call | solution.py:340
  33.8 1.0 %finish.1 = (f32[4,64,256]{2,1,0:T(8,128)}, f32[1,1]{1,0:T(1,128)}) custom-call(f32[1,128]{1,0:T(1,128)S(1)} %get-tuple-element.7.total_ref, f32[4,64,256]{2,1,0:T(8,128)S(1)} %get-tuple-element.8.image_ref, f32[4,64,256]{2,1,0:T(8,128)S(1)} %get-tuple-element.9.prob_ref), custom_call_target="tpu_custom_call" | custom-call | tf_op jit(solution)/shard_map/finish/pallas_call | solution.py:362

commit v4 on v3

--- a/solution.py
+++ b/solution.py
@@ -161,6 +161,9 @@
             sends.append(copy)
             return copy
 
+        obs_copies = [
+            send(w_send, w_recv.at[n], obs_send.at[n], obs_recv.at[n], dx, dy) for n, (dx, dy) in enumerate(cross)
+        ]
         coef_copies = [
             send(edge_v.at[m, rows - 8:rows] if n == 0 else edge_v.at[m, 0:8], diag_recv.at[n, m],
                  coef_send.at[4 + 2 * n + m], coef_recv.at[4 + 2 * n + m], 1 - 2 * n, 1 - 2 * m)
@@ -170,10 +173,6 @@
             for n in range(2)
         ] + [
             send(col_send.at[n], col_recv.at[n], coef_send.at[n], coef_recv.at[n], 0, 1 - 2 * n) for n in range(2)
-        ]
-
-        obs_copies = [
-            send(w_send, w_recv.at[n], obs_send.at[n], obs_recv.at[n], dx, dy) for n, (dx, dy) in enumerate(cross)
         ]
 
         row_ids, col_ids = iota((ext_r, ext_c), 0), iota((ext_r, ext_c), 1)
@@ -294,9 +293,12 @@
                 send(part.at[stage], got.at[d - 1], ssem.at[d - 1], rsem.at[d - 1], *((0, d) if stage == 0 else (d, 0)))
                 for d in range(1, size)
             ]
-            for d, copy in enumerate(copies):
+            for copy in copies:
                 copy.wait_recv()
-                total = total + got[d]
+            lines = [total] + [got[d] for d in range(size - 1)]
+            while len(lines) > 1:
+                lines = [lines[n] + lines[n + 1] for n in range(0, len(lines), 2)]
+            total = lines[0]
         total_ref[...] = total
         for save in saves:
             save.wait()

time: 34.9 us -> 34.9 us (level)
  no operation moved by 1% of the time
where the time goes in v4:
time: 34.9 us; the launch traced here: 34.7 us
  Pallas kernels  33.4 us (96%)
  between operations  1.29 us (4%)
    pallas_call x1, Pallas kernels, per_device(): pl.pallas_call(body, name='two_steps', out_shape=(field, field, jax.Shape...  32.5 us
    pallas_call x1, Pallas kernels, per_device(): pl.pallas_call(finish, name='finish', out_shape=(field, jax.ShapeDtypeStr...  0.96 us

profile of v4, /device:TPU:1, one launch (start us, length us, event | category | flops | bytes accessed | tf_op | source)
XLA Modules:
  0.0 34.7 jit_solution(6642546781101718447)
XLA Ops:
  1.3 32.5 %two_steps.1 = (f32[4,64,256]{2,1,0:T(8,128)S(1)}, f32[4,64,256]{2,1,0:T(8,128)S(1)}, f32[1,128]{1,0:T(1,128)S(1)}) custom-call(s32[1,4]{1,0:T(1,128)} %bitcast.6, f32[64,256]{1,0:T(8,128)} %damp_h.1, f32[64,256]{1,0:T(8,128)} %cx_h.1, f32[64,256]{1,0:T(8,128)} %cy_h.1, s32[1,1]{1,0:T(1,128)S(6)} %copy.9.count_s, s32[1,256]{1,0:T(1,128)} %bitcast.5, ...), custom_call_target="tpu_custom_call" | custom-call | tf_op jit(solution)/shard_map/two_steps/pallas_call | solution.py:342
  33.8 1.0 %finish.1 = (f32[4,64,256]{2,1,0:T(8,128)}, f32[1,1]{1,0:T(1,128)}) custom-call(f32[1,128]{1,0:T(1,128)S(1)} %get-tuple-element.7.total_ref, f32[4,64,256]{2,1,0:T(8,128)S(1)} %get-tuple-element.8.image_ref, f32[4,64,256]{2,1,0:T(8,128)S(1)} %get-tuple-element.9.prob_ref), custom_call_target="tpu_custom_call" | custom-call | tf_op jit(solution)/shard_map/finish/pallas_call | solution.py:364

commit v5 on v4

--- a/solution.py
+++ b/solution.py
@@ -259,8 +259,6 @@
         saves.append(pltpu.make_async_copy(inner_v, image_h, local_sem.at[7]))
         saves[1].start()
 
-        relay(0, 2)
-
         def fold(x):
             total = jnp.sum(x.reshape(rows // 8, 8, cols), axis=0)
             total = sum(total[:, n * 128:(n + 1) * 128] for n in range(cols // 128))
@@ -293,6 +291,8 @@
                 send(part.at[stage], got.at[d - 1], ssem.at[d - 1], rsem.at[d - 1], *((0, d) if stage == 0 else (d, 0)))
                 for d in range(1, size)
             ]
+            if stage == 0:
+                relay(0, 2)
             for copy in copies:
                 copy.wait_recv()
             lines = [total] + [got[d] for d in range(size - 1)]

time: 34.9 us -> 34.8 us (level)
  no operation moved by 1% of the time
where the time goes in v5:
time: 34.8 us; the launch traced here: 34.6 us
  Pallas kernels  33.4 us (96%)
  between operations  1.29 us (4%)
    pallas_call x1, Pallas kernels, per_device(): pl.pallas_call(body, name='two_steps', out_shape=(field, field, jax.Shape...  32.4 us
    pallas_call x1, Pallas kernels, per_device(): pl.pallas_call(finish, name='finish', out_shape=(field, jax.ShapeDtypeStr...  0.96 us

profile of v5, /device:TPU:1, one launch (start us, length us, event | category | flops | bytes accessed | tf_op | source)
XLA Modules:
  0.0 34.6 jit_solution(16205773024804048427)
XLA Ops:
  1.3 32.4 %two_steps.1 = (f32[4,64,256]{2,1,0:T(8,128)S(1)}, f32[4,64,256]{2,1,0:T(8,128)S(1)}, f32[1,128]{1,0:T(1,128)S(1)}) custom-call(s32[1,4]{1,0:T(1,128)} %bitcast.6, f32[64,256]{1,0:T(8,128)} %damp_h.1, f32[64,256]{1,0:T(8,128)} %cx_h.1, f32[64,256]{1,0:T(8,128)} %cy_h.1, s32[1,1]{1,0:T(1,128)S(6)} %copy.9.count_s, s32[1,256]{1,0:T(1,128)} %bitcast.5, ...), custom_call_target="tpu_custom_call" | custom-call | tf_op jit(solution)/shard_map/two_steps/pallas_call | solution.py:342
  33.7 1.0 %finish.1 = (f32[4,64,256]{2,1,0:T(8,128)}, f32[1,1]{1,0:T(1,128)}) custom-call(f32[1,128]{1,0:T(1,128)S(1)} %get-tuple-element.7.total_ref, f32[4,64,256]{2,1,0:T(8,128)S(1)} %get-tuple-element.8.image_ref, f32[4,64,256]{2,1,0:T(8,128)S(1)} %get-tuple-element.9.prob_ref), custom_call_target="tpu_custom_call" | custom-call | tf_op jit(solution)/shard_map/finish/pallas_call | solution.py:364
